TPU v7x, 32 devices: a whole 2x2x4 slice. The times are simulated.
32 devices in a mesh: blk: 8 (over z, y), grp: 4 (over x, core).
Axes of the slice: x: 2, y: 2, z: 4, core: 2. Of those that a mesh axis runs over, the one named last changes fastest.
Arguments:
- state: float32 [6, 131072], P(None, ('blk', 'grp')), may hold values from -6 to 6
- mass: float32 [131072], P(('blk', 'grp')), may hold values from 1.5258789e-06 to 3.8146973e-05
- active_index: int32 [8, 32], P('blk'), may hold values from 0 to 16383, as said below
- counts: int32 [8], P('blk'), may hold values from 8 to 32, as said below
Outputs:
- acc_jerk: float32 [6, 256], P(None, 'blk')
- potential: float32 [256], P('blk')
Inputs may be any that keep to these rules, and one draw needn't show every extreme that they name: `active_index`: each row holds 32 different star numbers of its slot block; only the first counts[b] entries of row b are active. `counts`: in every draw some slot is full, with 32 active stars.
All inputs are finite; a program needn't handle non-finite values.
Results may differ from a plain program's by a relative error of at most 0.0003.
Values sent between devices are 32-bit elements; how exact they have to be, the bound alone decides.
A program may use at most 64 MiB of HBM per device.

v0:
```python
import jax
import jax.numpy as jnp
from jax import lax
from jax.sharding import PartitionSpec as P

softening = 0.001


def shifted(block, axis, distance):
    devices = range(lax.axis_size(axis))
    route = [((i - distance) % len(devices), i) for i in devices]
    return lax.ppermute(block, axis, route)


def pair_terms(active, field):
    dpos = field[0:3, None, :] - active[0:3, :, None]
    dvel = field[3:6, None, :] - active[3:6, :, None]
    raw = jnp.sum(dpos * dpos, axis=0)
    weight = jnp.where(raw == 0.0, 0.0, field[6][None, :])
    inv = lax.rsqrt(raw + softening)
    first = weight * inv
    third = first * inv * inv
    along = jnp.sum(dpos * dvel, axis=0)
    fifth = 3.0 * along * third * inv * inv
    accel = jnp.sum(third[None] * dpos, axis=-1)
    jerk = jnp.sum(third[None] * dvel - fifth[None] * dpos, axis=-1)
    pot = -jnp.sum(first, axis=-1)
    return jnp.concatenate([accel, jerk, pot[None]], axis=0)


def live_terms(active, field):
    return pair_terms(active, field)


def on_device(state, mass, active_index, counts):
    blocks = lax.axis_size("blk")
    capacity = active_index.shape[1]
    picks = active_index[0]
    count_live = counts[0]
    slot_state = lax.all_gather(state, "grp", axis=1, tiled=True)
    active = jnp.take(slot_state, picks, axis=1)
    field = jnp.concatenate([state, mass[None, :]], axis=0)

    def turn_one(step, carry):
        summed, moving = carry
        moving = shifted(moving, "blk", 1)
        return (summed + live_terms(active, moving), moving)

    start = live_terms(active, field)
    total = lax.fori_loop(1, blocks, turn_one, (start, field))[0]
    live = jnp.arange(capacity, dtype=jnp.int32) < count_live
    total = jnp.where(live[None, :], total, 0.0)
    summed = lax.psum(total, "grp")
    return (summed[0:6], summed[6])


def solution(mesh):
    placed = (P(None, ("blk", "grp")), P(("blk", "grp")), P("blk", None), P("blk"))
    return jax.shard_map(
        on_device, mesh=mesh, in_specs=placed, out_specs=(P(None, "blk"), P("blk")), check_vma=False
    )
```

profile of v0, /device:TPU:0, one launch (start us, length us, event | category | flops | bytes accessed | tf_op | source)
XLA Modules:
  0.0 132.4 jit_solution(1626110730015682410)
XLA Ops:
  0.6 1.5 %copy.10 = f32[6,4096]{0,1:T(8,128)S(1)} copy(f32[6,4096]{1,0:T(8,128)} %param.6) | data formatting | bytes 196608 | tf_op args[0]
  2.2 52.0 %all_gather.3 = f32[6,16384]{0,1:T(8,128)} all-gather(f32[6,4096]{0,1:T(8,128)S(1)} %copy.10), channel_id=1, replica_groups=mesh['blk'=8,'grp'=4] {'grp'}, dimensions={1}, use_global_device_ids=true | all-gather | bytes 491520 | tf_op jit(solution)/shard_map/all_gather | solution.py:40
  54.3 4.0 %gather_fusion = f32[32,6]{1,0:T(8,128)S(1)} fusion(f32[6,16384]{0,1:T(8,128)} %all_gather.3, s32[1024]{0:T(1024)S(1)} %pad_clamp_fusion), kind=kCustom, calls=%fused_computation | custom fusion | bytes 1664 | tf_op jit(solution)/shard_map/jit(_take)/gather | solution.py:41
  58.6 0.4 fusion.10
  59.3 0.6 fusion.9
  60.1 65.4 %while.12 = (s32[]{:T(128)}, f32[7,32]{1,0:T(8,128)S(1)}, f32[7,4096]{1,0:T(8,128)S(1)}, f32[6,32]{1,0:T(8,128)S(1)}, s32[]{:T(128)}) while((s32[]{:T(128)}, f32[7,32]{1,0:T(8,128)S(1)}, f32[7,4096]{1,0:T(8,128)S(1)}, f32[6,32]{1,0:T(8,128)S(1)}, s32[]{:T(128)}) %tuple.46), condition=%wide.region_11.12_spmd, body=%wide.region_5.11_spmd.sunk | while | flops 6685154 | bytes 5331813 | solution.py:50
  60.1 1.6 %collective-permute-start = (f32[7,4096]{1,0:T(8,128)S(1)}, f32[7,4096]{1,0:T(8,128)S(1)}, u32[]{:S(2)}, u32[]{:S(2)}) collective-permute-start(f32[7,4096]{1,0:T(8,128)S(1)} %get-tuple-element.117), channel_id=1, source_target_pairs={{28,0},{0,4},{4,8},{8,12},{12,16},{16,20},{20,24},{24,28},{29,1},{... | collective-permute-start | bytes 344072 | tf_op jit(solution)/shard_map/while/body/eval_jaxpr/ppermute | solution.py:12
  61.7 7.1 %collective-permute-done = f32[7,4096]{1,0:T(8,128)S(1)} collective-permute-done((f32[7,4096]{1,0:T(8,128)S(1)}, f32[7,4096]{1,0:T(8,128)S(1)}, u32[]{:S(2)}, u32[]{:S(2)}) %collective-permute-start) | collective-permute-done | bytes 114720 | tf_op jit(solution)/shard_map/while/body/eval_jaxpr/ppermute | solution.py:12
  68.8 0.4 fusion.23
  69.5 0.6 fusion.24
  70.3 7.7 %collective-permute-done = f32[7,4096]{1,0:T(8,128)S(1)} collective-permute-done((f32[7,4096]{1,0:T(8,128)S(1)}, f32[7,4096]{1,0:T(8,128)S(1)}, u32[]{:S(2)}, u32[]{:S(2)}) %collective-permute-start) | collective-permute-done | bytes 114720 | tf_op jit(solution)/shard_map/while/body/eval_jaxpr/ppermute | solution.py:12
  78.8 0.6 fusion.24
  79.6 7.6 %collective-permute-done = f32[7,4096]{1,0:T(8,128)S(1)} collective-permute-done((f32[7,4096]{1,0:T(8,128)S(1)}, f32[7,4096]{1,0:T(8,128)S(1)}, u32[]{:S(2)}, u32[]{:S(2)}) %collective-permute-start) | collective-permute-done | bytes 114720 | tf_op jit(solution)/shard_map/while/body/eval_jaxpr/ppermute | solution.py:12
  88.0 0.6 fusion.24
  88.8 7.6 %collective-permute-done = f32[7,4096]{1,0:T(8,128)S(1)} collective-permute-done((f32[7,4096]{1,0:T(8,128)S(1)}, f32[7,4096]{1,0:T(8,128)S(1)}, u32[]{:S(2)}, u32[]{:S(2)}) %collective-permute-start) | collective-permute-done | bytes 114720 | tf_op jit(solution)/shard_map/while/body/eval_jaxpr/ppermute | solution.py:12
  97.2 0.6 fusion.24
  97.9 7.6 %collective-permute-done = f32[7,4096]{1,0:T(8,128)S(1)} collective-permute-done((f32[7,4096]{1,0:T(8,128)S(1)}, f32[7,4096]{1,0:T(8,128)S(1)}, u32[]{:S(2)}, u32[]{:S(2)}) %collective-permute-start) | collective-permute-done | bytes 114720 | tf_op jit(solution)/shard_map/while/body/eval_jaxpr/ppermute | solution.py:12
  106.4 0.6 fusion.24
  107.1 7.6 %collective-permute-done = f32[7,4096]{1,0:T(8,128)S(1)} collective-permute-done((f32[7,4096]{1,0:T(8,128)S(1)}, f32[7,4096]{1,0:T(8,128)S(1)}, u32[]{:S(2)}, u32[]{:S(2)}) %collective-permute-start) | collective-permute-done | bytes 114720 | tf_op jit(solution)/shard_map/while/body/eval_jaxpr/ppermute | solution.py:12
  115.6 0.6 fusion.24
  116.3 7.6 %collective-permute-done = f32[7,4096]{1,0:T(8,128)S(1)} collective-permute-done((f32[7,4096]{1,0:T(8,128)S(1)}, f32[7,4096]{1,0:T(8,128)S(1)}, u32[]{:S(2)}, u32[]{:S(2)}) %collective-permute-start) | collective-permute-done | bytes 114720 | tf_op jit(solution)/shard_map/while/body/eval_jaxpr/ppermute | solution.py:12
  124.8 0.6 fusion.24
  126.1 5.7 %psum.7 = f32[7,32]{1,0:T(8,128)S(1)} all-reduce(f32[7,32]{1,0:T(8,128)S(1)} %broadcast_select_fusion), channel_id=1, replica_groups=mesh['blk'=8,'grp'=4] {'grp'}, use_global_device_ids=true, to_apply=%region_12.13 | all-reduce | flops 224 | bytes 1792 | tf_op jit(solution)/shard_map/psum | solution.py:53
  131.8 0.5 slice_bitcast_fusion
  (84 shorter events, 6.5 us)
Async XLA Ops:
  2.2 52.1 %copy-start.3 = (s32[1,32]{1,0:T(1,128)S(1)}, s32[1,32]{1,0:T(1,128)}, u32[]{:S(2)}) copy-start(s32[1,32]{1,0:T(1,128)} %param.8) | copy-start | bytes 388
  2.2 56.3 %copy-start = (f32[6,4096]{1,0:T(8,128)S(1)}, f32[6,4096]{1,0:T(8,128)}, u32[]{:S(2)}) copy-start(f32[6,4096]{1,0:T(8,128)} %param.6) | copy-start | bytes 294916
  54.2 4.8 %copy-start.1 = (f32[4096]{0:T(1024)S(1)}, f32[4096]{0:T(1024)}, u32[]{:S(2)}) copy-start(f32[4096]{0:T(1024)} %param.7) | copy-start | bytes 49156
  60.1 8.6 %collective-permute-start = (f32[7,4096]{1,0:T(8,128)S(1)}, f32[7,4096]{1,0:T(8,128)S(1)}, u32[]{:S(2)}, u32[]{:S(2)}) collective-permute-start(f32[7,4096]{1,0:T(8,128)S(1)} %get-tuple-element.117), channel_id=1, source_target_pairs={{28,0},{0,4},{4,8},{8,12},{12,16},{16,20},{20,24},{24,28},{29,1},{... | collective-permute-start | bytes 344072 | tf_op jit(solution)/shard_map/while/body/eval_jaxpr/ppermute | solution.py:12
  70.2 7.8 %collective-permute-start = (f32[7,4096]{1,0:T(8,128)S(1)}, f32[7,4096]{1,0:T(8,128)S(1)}, u32[]{:S(2)}, u32[]{:S(2)}) collective-permute-start(f32[7,4096]{1,0:T(8,128)S(1)} %get-tuple-element.117), channel_id=1, source_target_pairs={{28,0},{0,4},{4,8},{8,12},{12,16},{16,20},{20,24},{24,28},{29,1},{... | collective-permute-start | bytes 344072 | tf_op jit(solution)/shard_map/while/body/eval_jaxpr/ppermute | solution.py:12
  79.5 7.7 %collective-permute-start = (f32[7,4096]{1,0:T(8,128)S(1)}, f32[7,4096]{1,0:T(8,128)S(1)}, u32[]{:S(2)}, u32[]{:S(2)}) collective-permute-start(f32[7,4096]{1,0:T(8,128)S(1)} %get-tuple-element.117), channel_id=1, source_target_pairs={{28,0},{0,4},{4,8},{8,12},{12,16},{16,20},{20,24},{24,28},{29,1},{... | collective-permute-start | bytes 344072 | tf_op jit(solution)/shard_map/while/body/eval_jaxpr/ppermute | solution.py:12
  88.7 7.7 %collective-permute-start = (f32[7,4096]{1,0:T(8,128)S(1)}, f32[7,4096]{1,0:T(8,128)S(1)}, u32[]{:S(2)}, u32[]{:S(2)}) collective-permute-start(f32[7,4096]{1,0:T(8,128)S(1)} %get-tuple-element.117), channel_id=1, source_target_pairs={{28,0},{0,4},{4,8},{8,12},{12,16},{16,20},{20,24},{24,28},{29,1},{... | collective-permute-start | bytes 344072 | tf_op jit(solution)/shard_map/while/body/eval_jaxpr/ppermute | solution.py:12
  97.9 7.7 %collective-permute-start = (f32[7,4096]{1,0:T(8,128)S(1)}, f32[7,4096]{1,0:T(8,128)S(1)}, u32[]{:S(2)}, u32[]{:S(2)}) collective-permute-start(f32[7,4096]{1,0:T(8,128)S(1)} %get-tuple-element.117), channel_id=1, source_target_pairs={{28,0},{0,4},{4,8},{8,12},{12,16},{16,20},{20,24},{24,28},{29,1},{... | collective-permute-start | bytes 344072 | tf_op jit(solution)/shard_map/while/body/eval_jaxpr/ppermute | solution.py:12
  107.1 7.7 %collective-permute-start = (f32[7,4096]{1,0:T(8,128)S(1)}, f32[7,4096]{1,0:T(8,128)S(1)}, u32[]{:S(2)}, u32[]{:S(2)}) collective-permute-start(f32[7,4096]{1,0:T(8,128)S(1)} %get-tuple-element.117), channel_id=1, source_target_pairs={{28,0},{0,4},{4,8},{8,12},{12,16},{16,20},{20,24},{24,28},{29,1},{... | collective-permute-start | bytes 344072 | tf_op jit(solution)/shard_map/while/body/eval_jaxpr/ppermute | solution.py:12
  116.3 7.7 %collective-permute-start = (f32[7,4096]{1,0:T(8,128)S(1)}, f32[7,4096]{1,0:T(8,128)S(1)}, u32[]{:S(2)}, u32[]{:S(2)}) collective-permute-start(f32[7,4096]{1,0:T(8,128)S(1)} %get-tuple-element.117), channel_id=1, source_target_pairs={{28,0},{0,4},{4,8},{8,12},{12,16},{16,20},{20,24},{24,28},{29,1},{... | collective-permute-start | bytes 344072 | tf_op jit(solution)/shard_map/while/body/eval_jaxpr/ppermute | solution.py:12
  131.8 0.6 copy-start.2
where the time goes:
time: 133 us; the launch traced here: 132 us
  blocking collectives  57.7 us (43%)
  waiting for transfers between devices  53 us (40%)
  other arithmetic  11.1 us (8%)
  local copies, waits for them, and re-layouts  6.87 us (5%)
  starting transfers between devices  1.92 us (1%)
  between operations  1.38 us (1%)
    ppermute x7, waiting for transfers between devices, shifted(): return lax.ppermute(block, axis, route)  53 us
    all_gather x1, blocking collectives, on_device(): slot_state = lax.all_gather(state, 'grp', axis=1, tiled=True)  52 us
    psum x1, blocking collectives, on_device(): summed = lax.psum(total, 'grp')  5.67 us
    reduce_sum x8, other arithmetic, pair_terms(): accel = jnp.sum(third[None] * dpos, axis=-1)  5.02 us
    gather x1, local copies, waits for them, and re-layouts, on_device(): active = jnp.take(slot_state, picks, axis=1)  3.95 us
    reduce_sum x8, other arithmetic, pair_terms(): along = jnp.sum(dpos * dvel, axis=0)  3.27 us
  transfers between devices with their start and end apart: 7, of which 7 were waited for; matrix products, arithmetic and copies ran while one was open for 0% of the time, Pallas kernels for 0%

commit v1 on v0

--- a/solution.py
+++ b/solution.py
@@ -37,7 +37,9 @@
     capacity = active_index.shape[1]
     picks = active_index[0]
     count_live = counts[0]
-    slot_state = lax.all_gather(state, "grp", axis=1, tiled=True)
+    slot_state = jnp.concatenate(
+        lax.all_to_all(jnp.stack([state] * lax.axis_size("grp")), "grp", 0, 0), axis=1
+    )
     active = jnp.take(slot_state, picks, axis=1)
     field = jnp.concatenate([state, mass[None, :]], axis=0)
 

time: 133 us -> 97.8 us (0.74)
  blocking collectives: 57.7 us -> 5.67 us
  waiting for transfers between devices: 53 us -> 60.1 us
  local copies, waits for them, and re-layouts: 6.87 us -> 12 us
  starting transfers between devices: 1.92 us -> 6.84 us
    all_gather x1 -> x0, blocking collectives: 52 us -> none  [on_device(): slot_state = lax.all_gather(state, 'grp', axis=1, tiled=True)]
    all_to_all x0 -> x1, waiting for transfers between devices: none -> 8.02 us  [on_device(): lax.all_to_all(jnp.stack([state] * lax.axis_size('grp')), 'grp', 0, 0)]
    reshape x0 -> x1, local copies, waits for them, and re-layouts: none -> 4.87 us  [on_device(): jnp.concatenate(lax.all_to_all(jnp.stack([state] * lax.axis_size('grp')),...]
    all_to_all x0 -> x1, starting transfers between devices: none -> 4.24 us  [on_device(): lax.all_to_all(jnp.stack([state] * lax.axis_size('grp')), 'grp', 0, 0)]
    another operation x0 -> x1, local copies, waits for them, and re-layouts: none -> 1.79 us  [on_device(): jnp.stack([state] * lax.axis_size('grp'))]
    unnamed x9 -> x8, local copies, waits for them, and re-layouts: 1.63 us -> 0.09 us
  transfers between devices with their start and end apart: 7 -> 8, of which waited for: 7 -> 8; matrix products, arithmetic and copies ran while one was open for 0% -> 0% of each run, Pallas kernels for 0% -> 0%
where the time goes in v1:
time: 97.8 us; the launch traced here: 97.5 us
  waiting for transfers between devices  60.1 us (61%)
  local copies, waits for them, and re-layouts  12 us (12%)
  other arithmetic  11.1 us (11%)
  starting transfers between devices  6.84 us (7%)
  blocking collectives  5.67 us (6%)
  between operations  1.39 us (1%)
    ppermute x7, waiting for transfers between devices, shifted(): return lax.ppermute(block, axis, route)  52.1 us
    all_to_all x1, waiting for transfers between devices, on_device(): lax.all_to_all(jnp.stack([state] * lax.axis_size('grp')), 'grp', 0, 0)  8.02 us
    psum x1, blocking collectives, on_device(): summed = lax.psum(total, 'grp')  5.67 us
    reduce_sum x8, other arithmetic, pair_terms(): accel = jnp.sum(third[None] * dpos, axis=-1)  5.02 us
    reshape x1, local copies, waits for them, and re-layouts, on_device(): jnp.concatenate(lax.all_to_all(jnp.stack([state] * lax.axis_size('grp')),...  4.87 us
    all_to_all x1, starting transfers between devices, on_device(): lax.all_to_all(jnp.stack([state] * lax.axis_size('grp')), 'grp', 0, 0)  4.24 us
    gather x1, local copies, waits for them, and re-layouts, on_device(): active = jnp.take(slot_state, picks, axis=1)  3.95 us
    reduce_sum x8, other arithmetic, pair_terms(): along = jnp.sum(dpos * dvel, axis=0)  3.29 us
  transfers between devices with their start and end apart: 8, of which 8 were waited for; matrix products, arithmetic and copies ran while one was open for 0% of the time, Pallas kernels for 0%

profile of v1, /device:TPU:0, one launch (start us, length us, event | category | flops | bytes accessed | tf_op | source)
XLA Modules:
  0.0 97.5 jit_solution(11140325787586992840)
XLA Ops:
  0.7 1.8 %stack.2 = f32[4,6,4096]{2,1,0:T(8,128)} broadcast(f32[6,4096]{1,0:T(8,128)} %param.6), dimensions={1,2} | broadcast | bytes 491520 | tf_op jit(solution)/shard_map/stack | solution.py:41
  2.5 4.2 %all-to-all-start = ((f32[4,6,4096]{2,1,0:T(8,128)}), f32[4,6,4096]{2,1,0:T(8,128)S(1)}, u32[]{:S(2)}, u32[]{:S(2)}) async-start(f32[4,6,4096]{2,1,0:T(8,128)} %stack.2), calls=%async_computation | async-start | bytes 1048576 | tf_op jit(solution)/shard_map/all_to_all | solution.py:41
  7.5 8.0 %all-to-all-done = f32[4,6,4096]{2,1,0:T(8,128)S(1)} async-done(((f32[4,6,4096]{2,1,0:T(8,128)}), f32[4,6,4096]{2,1,0:T(8,128)S(1)}, u32[]{:S(2)}, u32[]{:S(2)}) %all-to-all-start) | async-done | bytes 393248 | tf_op jit(solution)/shard_map/all_to_all | solution.py:41
  15.5 4.9 %copy.14 = f32[6,4,4096]{0,2,1:T(8,128)} copy(f32[6,4,4096]{2,0,1:T(8,128)S(1)} %bitcast.26) | data formatting | bytes 786432 | tf_op jit(solution)/shard_map/reshape | solution.py:40
  20.4 4.0 %gather_fusion = f32[32,6]{1,0:T(8,128)S(1)} fusion(f32[6,16384]{0,1:T(8,128)} %bitcast.25, s32[1024]{0:T(1024)S(1)} %pad_clamp_fusion), kind=kCustom, calls=%fused_computation | custom fusion | bytes 1664 | tf_op jit(solution)/shard_map/jit(_take)/gather | solution.py:43
  25.5 0.6 fusion.9
  26.1 65.1 %while.12 = (s32[]{:T(128)}, f32[7,32]{1,0:T(8,128)S(1)}, f32[7,4096]{1,0:T(8,128)S(1)}, f32[6,32]{1,0:T(8,128)S(1)}, s32[]{:T(128)}) while((s32[]{:T(128)}, f32[7,32]{1,0:T(8,128)S(1)}, f32[7,4096]{1,0:T(8,128)S(1)}, f32[6,32]{1,0:T(8,128)S(1)}, s32[]{:T(128)}) %tuple.47), condition=%wide.region_11.12_spmd, body=%wide.region_5.11_spmd.sunk | while | flops 6685154 | bytes 5331813 | solution.py:52
  26.1 2.3 %collective-permute-start = (f32[7,4096]{1,0:T(8,128)S(1)}, f32[7,4096]{1,0:T(8,128)S(1)}, u32[]{:S(2)}, u32[]{:S(2)}) collective-permute-start(f32[7,4096]{1,0:T(8,128)S(1)} %get-tuple-element.121), channel_id=1, source_target_pairs={{28,0},{0,4},{4,8},{8,12},{12,16},{16,20},{20,24},{24,28},{29,1},{... | collective-permute-start | bytes 344072 | tf_op jit(solution)/shard_map/while/body/eval_jaxpr/ppermute | solution.py:12
  28.4 6.2 %collective-permute-done = f32[7,4096]{1,0:T(8,128)S(1)} collective-permute-done((f32[7,4096]{1,0:T(8,128)S(1)}, f32[7,4096]{1,0:T(8,128)S(1)}, u32[]{:S(2)}, u32[]{:S(2)}) %collective-permute-start) | collective-permute-done | bytes 114720 | tf_op jit(solution)/shard_map/while/body/eval_jaxpr/ppermute | solution.py:12
  35.4 0.6 fusion.24
  36.2 7.6 %collective-permute-done = f32[7,4096]{1,0:T(8,128)S(1)} collective-permute-done((f32[7,4096]{1,0:T(8,128)S(1)}, f32[7,4096]{1,0:T(8,128)S(1)}, u32[]{:S(2)}, u32[]{:S(2)}) %collective-permute-start) | collective-permute-done | bytes 114720 | tf_op jit(solution)/shard_map/while/body/eval_jaxpr/ppermute | solution.py:12
  44.6 0.6 fusion.24
  45.4 7.6 %collective-permute-done = f32[7,4096]{1,0:T(8,128)S(1)} collective-permute-done((f32[7,4096]{1,0:T(8,128)S(1)}, f32[7,4096]{1,0:T(8,128)S(1)}, u32[]{:S(2)}, u32[]{:S(2)}) %collective-permute-start) | collective-permute-done | bytes 114720 | tf_op jit(solution)/shard_map/while/body/eval_jaxpr/ppermute | solution.py:12
  53.8 0.6 fusion.24
  54.6 7.6 %collective-permute-done = f32[7,4096]{1,0:T(8,128)S(1)} collective-permute-done((f32[7,4096]{1,0:T(8,128)S(1)}, f32[7,4096]{1,0:T(8,128)S(1)}, u32[]{:S(2)}, u32[]{:S(2)}) %collective-permute-start) | collective-permute-done | bytes 114720 | tf_op jit(solution)/shard_map/while/body/eval_jaxpr/ppermute | solution.py:12
  63.0 0.6 fusion.24
  63.7 7.6 %collective-permute-done = f32[7,4096]{1,0:T(8,128)S(1)} collective-permute-done((f32[7,4096]{1,0:T(8,128)S(1)}, f32[7,4096]{1,0:T(8,128)S(1)}, u32[]{:S(2)}, u32[]{:S(2)}) %collective-permute-start) | collective-permute-done | bytes 114720 | tf_op jit(solution)/shard_map/while/body/eval_jaxpr/ppermute | solution.py:12
  72.2 0.6 fusion.24
  72.9 7.6 %collective-permute-done = f32[7,4096]{1,0:T(8,128)S(1)} collective-permute-done((f32[7,4096]{1,0:T(8,128)S(1)}, f32[7,4096]{1,0:T(8,128)S(1)}, u32[]{:S(2)}, u32[]{:S(2)}) %collective-permute-start) | collective-permute-done | bytes 114720 | tf_op jit(solution)/shard_map/while/body/eval_jaxpr/ppermute | solution.py:12
  81.4 0.6 fusion.24
  82.1 7.6 %collective-permute-done = f32[7,4096]{1,0:T(8,128)S(1)} collective-permute-done((f32[7,4096]{1,0:T(8,128)S(1)}, f32[7,4096]{1,0:T(8,128)S(1)}, u32[]{:S(2)}, u32[]{:S(2)}) %collective-permute-start) | collective-permute-done | bytes 114720 | tf_op jit(solution)/shard_map/while/body/eval_jaxpr/ppermute | solution.py:12
  90.6 0.6 fusion.24
  91.3 5.7 %psum.7 = f32[7,32]{1,0:T(8,128)S(1)} all-reduce(f32[7,32]{1,0:T(8,128)S(1)} %broadcast_select_fusion), channel_id=1, replica_groups=mesh['blk'=8,'grp'=4] {'grp'}, use_global_device_ids=true, to_apply=%region_12.13 | all-reduce | flops 224 | bytes 1792 | tf_op jit(solution)/shard_map/psum | solution.py:55
  96.9 0.5 slice_bitcast_fusion
  (86 shorter events, 7.3 us)
Async XLA Ops:
  0.6 6.1 %copy-start = (f32[6,4096]{1,0:T(8,128)S(1)}, f32[6,4096]{1,0:T(8,128)}, u32[]{:S(2)}) copy-start(f32[6,4096]{1,0:T(8,128)} %param.6) | copy-start | bytes 294916
  0.6 6.1 %copy-start.3 = (s32[1,32]{1,0:T(1,128)S(1)}, s32[1,32]{1,0:T(1,128)}, u32[]{:S(2)}) copy-start(s32[1,32]{1,0:T(1,128)} %param.8) | copy-start | bytes 388
  0.6 6.1 %copy-start.1 = (f32[4096]{0:T(1024)S(1)}, f32[4096]{0:T(1024)}, u32[]{:S(2)}) copy-start(f32[4096]{0:T(1024)} %param.7) | copy-start | bytes 49156
  2.5 13.1 %all-to-all-start = ((f32[4,6,4096]{2,1,0:T(8,128)}), f32[4,6,4096]{2,1,0:T(8,128)S(1)}, u32[]{:S(2)}, u32[]{:S(2)}) async-start(f32[4,6,4096]{2,1,0:T(8,128)} %stack.2), calls=%async_computation | async-start | bytes 1048576 | tf_op jit(solution)/shard_map/all_to_all | solution.py:41
  26.1 8.5 %collective-permute-start = (f32[7,4096]{1,0:T(8,128)S(1)}, f32[7,4096]{1,0:T(8,128)S(1)}, u32[]{:S(2)}, u32[]{:S(2)}) collective-permute-start(f32[7,4096]{1,0:T(8,128)S(1)} %get-tuple-element.121), channel_id=1, source_target_pairs={{28,0},{0,4},{4,8},{8,12},{12,16},{16,20},{20,24},{24,28},{29,1},{... | collective-permute-start | bytes 344072 | tf_op jit(solution)/shard_map/while/body/eval_jaxpr/ppermute | solution.py:12
  36.1 7.7 %collective-permute-start = (f32[7,4096]{1,0:T(8,128)S(1)}, f32[7,4096]{1,0:T(8,128)S(1)}, u32[]{:S(2)}, u32[]{:S(2)}) collective-permute-start(f32[7,4096]{1,0:T(8,128)S(1)} %get-tuple-element.121), channel_id=1, source_target_pairs={{28,0},{0,4},{4,8},{8,12},{12,16},{16,20},{20,24},{24,28},{29,1},{... | collective-permute-start | bytes 344072 | tf_op jit(solution)/shard_map/while/body/eval_jaxpr/ppermute | solution.py:12
  45.3 7.7 %collective-permute-start = (f32[7,4096]{1,0:T(8,128)S(1)}, f32[7,4096]{1,0:T(8,128)S(1)}, u32[]{:S(2)}, u32[]{:S(2)}) collective-permute-start(f32[7,4096]{1,0:T(8,128)S(1)} %get-tuple-element.121), channel_id=1, source_target_pairs={{28,0},{0,4},{4,8},{8,12},{12,16},{16,20},{20,24},{24,28},{29,1},{... | collective-permute-start | bytes 344072 | tf_op jit(solution)/shard_map/while/body/eval_jaxpr/ppermute | solution.py:12
  54.5 7.7 %collective-permute-start = (f32[7,4096]{1,0:T(8,128)S(1)}, f32[7,4096]{1,0:T(8,128)S(1)}, u32[]{:S(2)}, u32[]{:S(2)}) collective-permute-start(f32[7,4096]{1,0:T(8,128)S(1)} %get-tuple-element.121), channel_id=1, source_target_pairs={{28,0},{0,4},{4,8},{8,12},{12,16},{16,20},{20,24},{24,28},{29,1},{... | collective-permute-start | bytes 344072 | tf_op jit(solution)/shard_map/while/body/eval_jaxpr/ppermute | solution.py:12
  63.7 7.7 %collective-permute-start = (f32[7,4096]{1,0:T(8,128)S(1)}, f32[7,4096]{1,0:T(8,128)S(1)}, u32[]{:S(2)}, u32[]{:S(2)}) collective-permute-start(f32[7,4096]{1,0:T(8,128)S(1)} %get-tuple-element.121), channel_id=1, source_target_pairs={{28,0},{0,4},{4,8},{8,12},{12,16},{16,20},{20,24},{24,28},{29,1},{... | collective-permute-start | bytes 344072 | tf_op jit(solution)/shard_map/while/body/eval_jaxpr/ppermute | solution.py:12
  72.9 7.7 %collective-permute-start = (f32[7,4096]{1,0:T(8,128)S(1)}, f32[7,4096]{1,0:T(8,128)S(1)}, u32[]{:S(2)}, u32[]{:S(2)}) collective-permute-start(f32[7,4096]{1,0:T(8,128)S(1)} %get-tuple-element.121), channel_id=1, source_target_pairs={{28,0},{0,4},{4,8},{8,12},{12,16},{16,20},{20,24},{24,28},{29,1},{... | collective-permute-start | bytes 344072 | tf_op jit(solution)/shard_map/while/body/eval_jaxpr/ppermute | solution.py:12
  82.1 7.7 %collective-permute-start = (f32[7,4096]{1,0:T(8,128)S(1)}, f32[7,4096]{1,0:T(8,128)S(1)}, u32[]{:S(2)}, u32[]{:S(2)}) collective-permute-start(f32[7,4096]{1,0:T(8,128)S(1)} %get-tuple-element.121), channel_id=1, source_target_pairs={{28,0},{0,4},{4,8},{8,12},{12,16},{16,20},{20,24},{24,28},{29,1},{... | collective-permute-start | bytes 344072 | tf_op jit(solution)/shard_map/while/body/eval_jaxpr/ppermute | solution.py:12
  96.9 0.6 copy-start.2
